TPU v7x, 512 devices: a whole 4x4x16 slice. The times are simulated.
512 devices in a mesh: row: 16 (over x, z_hi, core), col: 32 (over y, z_lo).
Axes of the slice: x: 4, y: 4, z: 16 (z_hi: 2, z_lo: 8; z = z_hi * 8 + z_lo), core: 2. Of those that a mesh axis runs over, the one named last changes fastest.
Arguments:
- a_blocks: float32 [384, 16, 128, 128], P('col', 'row'), may hold values from -0.25 to 0.25
- a_cols: int32 [384, 16], P('col'), may hold values from 0 to 63, as said below
- a_lengths: int32 [384], P('col'), may hold values from 1 to 16, as said below
- b_blocks: float32 [64, 16, 128, 128], P('col', 'row'), may hold values from -6 to 6
- b_cols: int32 [64, 16], P(None, 'row'), may hold values from 0 to 7
- c_cols: int32 [384, 64], P('col', 'row'), may hold values from 0 to 7, as said below
- order: int32 [64], replicated, may hold values from 0 to 63, each once
Outputs:
- c_blocks: float32 [384, 64, 128, 128], P('col', 'row')
Inputs may be any that keep to these rules, and one draw needn't show every extreme that they name: `a_cols`: the 16 entries of one row are distinct. `a_lengths`: the first row has 16 live slots; slots at or after a row's length hold blocks that are not used. `c_cols`: the 4 entries of one row in one row group are distinct. `order`: each number once.
All inputs are finite; a program needn't handle non-finite values.
Results may differ from a plain program's by a relative error of at most 0.0003.
Values sent between devices are 32-bit elements; how exact they have to be, the bound alone decides.
No kernel may reach another device: no remote copies, remote signals or barrier semaphores. Data moves between devices by JAX's collectives and lax.ppermute only.
A program may use at most 64 MiB of HBM per device.

v0:
```python
import jax
import jax.numpy as jnp
from jax import lax
from jax.sharding import PartitionSpec as P


def lookup(values_table, indices):
    matched = indices[..., None] == jnp.arange(values_table.shape[0], dtype=jnp.int32)
    return jnp.sum(jnp.where(matched, values_table, 0), axis=-1)


def local(a_blocks, a_cols, a_lengths, b_blocks, b_cols, c_cols, order):
    panels = lax.all_gather(b_blocks, "col", axis=0, tiled=True)[:, 0]
    rows_here, slot_all = a_cols.shape
    pattern_slots = c_cols.shape[1]
    block_size = panels.shape[-1]
    position = lookup(order, a_cols)
    window_col = lookup(b_cols[:, 0], position)
    live_slots = jnp.arange(slot_all, dtype=jnp.int32)[None, :] < a_lengths[:, None]
    weights = ((window_col[:, :, None] == c_cols[:, None, :]) & live_slots[:, :, None]).astype(
        jnp.float32
    )
    zero_sums = jnp.zeros((rows_here, pattern_slots, block_size, block_size), jnp.float32)
    whole_slots = lax.all_gather(a_blocks, "row", axis=1, tiled=True)

    def per_row(row_index, running):
        chosen = jnp.take(panels, position[row_index], axis=0)
        products = jnp.einsum(
            "jab,jbc->jac", whole_slots[row_index], chosen, precision=lax.Precision.HIGHEST
        )
        landed = jnp.einsum(
            "js,jac->sac", weights[row_index], products, precision=lax.Precision.HIGHEST
        )
        return running.at[row_index].add(landed)

    return lax.fori_loop(0, rows_here, per_row, zero_sums)


def solution(mesh):
    return jax.shard_map(
        local,
        mesh=mesh,
        in_specs=(
            P("col", "row", None, None),
            P("col", None),
            P("col"),
            P("col", "row", None, None),
            P(None, "row"),
            P("col", "row"),
            P(),
        ),
        out_specs=P("col", "row", None, None),
        check_vma=False,
    )
```

profile of v0, /device:TPU:105, one launch (start us, length us, event | category | flops | bytes accessed | tf_op | source)
XLA Modules:
  0.0 615.6 jit_solution(10681453512464985414)
XLA Ops:
  8.0 0.8 copy.14
  8.8 1.1 select_reduce_fusion.1
  9.8 1.0 select_reduce_fusion
  10.9 0.7 iota_compare_fusion.2
  11.7 190.3 %all-gather.5.cloned.1.call-done = f32[64,1,128,128]{3,2,1,0:T(8,128)} async-done(((f32[2,1,128,128]{3,2,1,0:T(8,128)}), f32[64,1,128,128]{3,2,1,0:T(8,128)}) %all-gather.5.cloned.1.call-update) | async-done | bytes 4194320 | tf_op jit(solution)/shard_map/all_gather | solution.py:13
  202.0 290.2 %all-gather.3.cloned.1.call-done = f32[12,16,128,128]{3,2,1,0:T(8,128)} async-done(((f32[12,1,128,128]{3,2,1,0:T(8,128)}), f32[12,16,128,128]{3,2,1,0:T(8,128)}) %all-gather.3.cloned.1.call-update) | async-done | bytes 12582928 | tf_op jit(solution)/shard_map/all_gather | solution.py:24
  492.2 2.0 broadcast_in_dim.47.clone
  494.3 114.5 %while.14 = (s32[]{:T(128)}, f32[12,4,128,128]{3,2,1,0:T(8,128)}, f32[12,16,4]{1,2,0:T(4,128)S(1)}, f32[12,16,128,128]{3,2,1,0:T(8,128)}, s32[12,16]{1,0:T(8,128...) while((s32[]{:T(128)}, f32[12,4,128,128]{3,2,1,0:T(8,128)}, ...), condition=%wide.region_4.5_spmd, body=%wide.region_2.4_spmd.sunk | while | flops 415630528 | bytes 7871975 | solution.py:36
  494.3 2.8 gather_fusion
  497.1 2.4 fusion.27
  500.3 1.0 constant_dynamic-slice_fusion.3
  501.2 1.8 fusion.28
  503.1 0.7 copy_dynamic-update-slice_fusion.2
  503.8 2.8 gather_fusion
  506.7 2.4 fusion.27
  509.8 1.0 constant_dynamic-slice_fusion.3
  510.8 1.8 fusion.28
  512.6 0.7 copy_dynamic-update-slice_fusion.2
  513.4 2.8 gather_fusion
  516.2 2.4 fusion.27
  519.3 1.0 constant_dynamic-slice_fusion.3
  520.3 1.8 fusion.28
  522.2 0.7 copy_dynamic-update-slice_fusion.2
  522.9 2.8 gather_fusion
  525.7 2.4 fusion.27
  528.9 1.0 constant_dynamic-slice_fusion.3
  529.9 1.8 fusion.28
  531.7 0.7 copy_dynamic-update-slice_fusion.2
  532.5 2.8 gather_fusion
  535.3 2.4 fusion.27
  538.4 1.0 constant_dynamic-slice_fusion.3
  539.4 1.8 fusion.28
  541.2 0.7 copy_dynamic-update-slice_fusion.2
  542.0 2.8 gather_fusion
  544.8 2.4 fusion.27
  548.0 1.0 constant_dynamic-slice_fusion.3
  548.9 1.8 fusion.28
  550.8 0.7 copy_dynamic-update-slice_fusion.2
  551.5 2.8 gather_fusion
  554.4 2.4 fusion.27
  557.5 1.0 constant_dynamic-slice_fusion.3
  558.5 1.8 fusion.28
  560.3 0.7 copy_dynamic-update-slice_fusion.2
  561.1 2.8 gather_fusion
  563.9 2.4 fusion.27
  567.0 1.0 constant_dynamic-slice_fusion.3
  568.0 1.8 fusion.28
  569.9 0.7 copy_dynamic-update-slice_fusion.2
  570.6 2.8 gather_fusion
  573.4 2.4 fusion.27
  576.6 1.0 constant_dynamic-slice_fusion.3
  577.6 1.8 fusion.28
  580.2 2.8 gather_fusion
  583.0 2.4 fusion.27
  586.1 1.0 constant_dynamic-slice_fusion.3
  587.1 1.8 fusion.28
  589.7 2.8 gather_fusion
  592.5 2.4 fusion.27
  595.7 1.0 constant_dynamic-slice_fusion.3
  596.6 1.8 fusion.28
  599.2 2.8 gather_fusion
  602.1 2.4 fusion.27
  605.2 1.0 constant_dynamic-slice_fusion.3
  606.2 1.8 fusion.28
  (59 shorter events, 13.3 us)
Async XLA Ops:
  6.5 487.7 %copy-start = (s32[4]{0:T(128)S(1)}, s32[4]{0:T(128)}, u32[]{:S(2)}) copy-start(s32[4]{0:T(128)} %constant.90.clone.1) | copy-start | bytes 52
  6.5 195.5 %all-gather.5.cloned.1.call-start = ((), (), s32[]{:S(2)}) async-start(), calls=%async_computation.1 | async-start | bytes 4325376 | tf_op jit(solution)/shard_map/all_gather | solution.py:13
  7.3 485.0 %all-gather.3.cloned.1.call-start = ((), (), s32[]{:S(2)}) async-start(), calls=%async_computation | async-start | bytes 13369344 | tf_op jit(solution)/shard_map/all_gather | solution.py:24
Sparse Core Ops, SparseCore 0:
  9.4 192.5 all-gather.4
  205.3 286.8 all-gather.2
where the time goes:
time: 617 us; the launch traced here: 616 us
  waiting for transfers between devices  482 us (78%)
  local copies, waits for them, and re-layouts  56.7 us (9%)
  matrix products  51.2 us (8%)
  between operations  13.4 us (2%)
  other arithmetic  11.8 us (2%)
    all_gather x1, waiting for transfers between devices, local(): whole_slots = lax.all_gather(a_blocks, 'row', axis=1, tiled=True)  290 us
    all_gather x1, waiting for transfers between devices, local(): panels = lax.all_gather(b_blocks, 'col', axis=0, tiled=True)[:, 0]  190 us
    gather x12, local copies, waits for them, and re-layouts, per_row(): chosen = jnp.take(panels, position[row_index], axis=0)  33.6 us
    dot_general x12, matrix products, per_row(): jnp.einsum('jab,jbc->jac', whole_slots[row_index], chosen, precision=lax....  29.1 us
    dot_general x12, matrix products, per_row(): jnp.einsum('js,jac->sac', weights[row_index], products, precision=lax.Pre...  22.2 us
  transfers between devices with their start and end apart: 2, of which 2 were waited for; matrix products, arithmetic and copies ran while one was open for 1% of the time, Pallas kernels for 0%

commit v1 on v0

--- a/solution.py
+++ b/solution.py
@@ -21,7 +21,9 @@
         jnp.float32
     )
     zero_sums = jnp.zeros((rows_here, pattern_slots, block_size, block_size), jnp.float32)
-    whole_slots = lax.all_gather(a_blocks, "row", axis=1, tiled=True)
+    whole_slots = jnp.concatenate(
+        lax.all_to_all(jnp.stack([a_blocks] * lax.axis_size("row")), "row", 0, 0), axis=1
+    )
 
     def per_row(row_index, running):
         chosen = jnp.take(panels, position[row_index], axis=0)

time: 617 us -> 800 us (1.30)
  the two profiles are of different devices: /device:TPU:105 before, /device:TPU:98 now
where the time goes in v1:
time: 800 us; the launch traced here: 798 us
  waiting for transfers between devices  643 us (80%)
  local copies, waits for them, and re-layouts  63.3 us (8%)
  matrix products  52.1 us (7%)
  starting transfers between devices  15.6 us (2%)
  between operations  13.5 us (2%)
  other arithmetic  10.2 us (1%)
    all_gather x1, waiting for transfers between devices, local(): panels = lax.all_gather(b_blocks, 'col', axis=0, tiled=True)[:, 0]  342 us
    all_to_all x1, waiting for transfers between devices, local(): lax.all_to_all(jnp.stack([a_blocks] * lax.axis_size('row')), 'row', 0, 0)  301 us
    gather x12, local copies, waits for them, and re-layouts, per_row(): chosen = jnp.take(panels, position[row_index], axis=0)  33.6 us
    dot_general x12, matrix products, per_row(): jnp.einsum('jab,jbc->jac', whole_slots[row_index], chosen, precision=lax....  29.1 us
    dot_general x12, matrix products, per_row(): jnp.einsum('js,jac->sac', weights[row_index], products, precision=lax.Pre...  23 us
  transfers between devices with their start and end apart: 2, of which 2 were waited for; matrix products, arithmetic and copies ran while one was open for 0% of the time, Pallas kernels for 0%

profile of v1, /device:TPU:98, one launch (start us, length us, event | category | flops | bytes accessed | tf_op | source)
XLA Modules:
  0.0 798.4 jit_solution(12758399397996000306)
XLA Ops:
  6.5 7.2 stack.2
  13.7 15.5 %all-to-all-start = ((f32[16,12,1,128,128]{4,3,1,2,0:T(8,128)}), f32[16,12,1,128,128]{4,3,1,2,0:T(8,128)}, u32[]{:S(2)}, u32[]{:S(2)}) async-start(f32[16,12,1,128,128]{4,3,1,2,0:T(8,128)} %stack.2), calls=%async_computation | async-start | bytes 25165824 | tf_op jit(solution)/shard_map/all_to_all | solution.py:25
  31.0 342.0 %all-gather.2.cloned.1.call-done = f32[64,1,128,128]{3,2,1,0:T(8,128)} async-done(((f32[2,1,128,128]{3,2,1,0:T(8,128)}), f32[64,1,128,128]{3,2,1,0:T(8,128)}) %all-gather.2.cloned.1.call-update) | async-done | bytes 4194320 | tf_op jit(solution)/shard_map/all_gather | solution.py:13
  373.0 300.7 %all-to-all-done = f32[16,12,1,128,128]{4,3,1,2,0:T(8,128)} async-done(((f32[16,12,1,128,128]{4,3,1,2,0:T(8,128)}), f32[16,12,1,128,128]{4,3,1,2,0:T(8,128)}, u32[]{:S(2)}, u32[]{:S(2)}) %all-to-all-start) | async-done | bytes 12582944 | tf_op jit(solution)/shard_map/all_to_all | solution.py:25
  673.7 2.0 broadcast_in_dim.47.clone
  675.7 115.8 %while.14 = (s32[]{:T(128)}, f32[12,4,128,128]{3,2,1,0:T(8,128)}, f32[12,16,4]{1,2,0:T(4,128)S(1)}, f32[12,16,128,128]{3,2,0,1:T(8,128)}, s32[12,16]{1,0:T(8,128...) while((s32[]{:T(128)}, f32[12,4,128,128]{3,2,1,0:T(8,128)}, ...), condition=%wide.region_4.5_spmd, body=%wide.region_2.4_spmd.sunk | while | flops 415630528 | bytes 7871975 | solution.py:38
  675.8 2.8 gather_fusion
  678.6 2.4 fusion.27
  681.0 0.7 and_reduce_fusion.2
  681.8 1.0 constant_dynamic-slice_fusion.3
  682.8 1.9 fusion.28
  685.4 2.8 gather_fusion
  688.3 2.4 fusion.27
  690.7 0.7 and_reduce_fusion.2
  691.4 1.0 constant_dynamic-slice_fusion.3
  692.4 1.9 fusion.28
  695.1 2.8 gather_fusion
  697.9 2.4 fusion.27
  700.3 0.7 and_reduce_fusion.2
  701.1 1.0 constant_dynamic-slice_fusion.3
  702.1 1.9 fusion.28
  704.7 2.8 gather_fusion
  707.6 2.4 fusion.27
  710.0 0.7 and_reduce_fusion.2
  710.7 1.0 constant_dynamic-slice_fusion.3
  711.7 1.9 fusion.28
  714.4 2.8 gather_fusion
  717.2 2.4 fusion.27
  719.6 0.7 and_reduce_fusion.2
  720.4 1.0 constant_dynamic-slice_fusion.3
  721.4 1.9 fusion.28
  724.0 2.8 gather_fusion
  726.9 2.4 fusion.27
  729.3 0.7 and_reduce_fusion.2
  730.0 1.0 constant_dynamic-slice_fusion.3
  731.0 1.9 fusion.28
  733.7 2.8 gather_fusion
  736.5 2.4 fusion.27
  738.9 0.7 and_reduce_fusion.2
  739.7 1.0 constant_dynamic-slice_fusion.3
  740.7 1.9 fusion.28
  743.3 2.8 gather_fusion
  746.2 2.4 fusion.27
  748.6 0.7 and_reduce_fusion.2
  749.3 1.0 constant_dynamic-slice_fusion.3
  750.3 1.9 fusion.28
  753.0 2.8 gather_fusion
  755.8 2.4 fusion.27
  758.2 0.7 and_reduce_fusion.2
  759.0 1.0 constant_dynamic-slice_fusion.3
  760.0 1.9 fusion.28
  762.6 2.8 gather_fusion
  765.5 2.4 fusion.27
  767.9 0.7 and_reduce_fusion.2
  768.6 1.0 constant_dynamic-slice_fusion.3
  769.6 1.9 fusion.28
  772.3 2.8 gather_fusion
  775.1 2.4 fusion.27
  778.3 1.0 constant_dynamic-slice_fusion.3
  779.3 1.9 fusion.28
  781.9 2.8 gather_fusion
  784.8 2.4 fusion.27
  787.9 1.0 constant_dynamic-slice_fusion.3
  788.9 1.9 fusion.28
  (69 shorter events, 12.3 us)
Async XLA Ops:
  13.7 16.3 %copy-start.2 = (s32[12,4]{0,1:T(4,128)S(1)}, s32[12,4]{0,1:T(4,128)}, u32[]{:S(2)}) copy-start(s32[12,4]{0,1:T(4,128)} %param.16) | copy-start | bytes 580
  13.7 16.4 %copy-start.1 = (s32[12,16]{1,0:T(8,128)S(1)}, s32[12,16]{1,0:T(8,128)}, u32[]{:S(2)}) copy-start(s32[12,16]{1,0:T(8,128)} %param.12) | copy-start | bytes 2308
  13.7 16.4 %copy-start.3 = (s32[64]{0:T(128)S(1)}, s32[64]{0:T(128)}, u32[]{:S(2)}) copy-start(s32[64]{0:T(128)} %param.17) | copy-start | bytes 772
  13.7 16.8 %copy-start.4 = (s32[64,1]{0,1:T(1,128)S(1)}, s32[64,1]{0,1:T(1,128)}, u32[]{:S(2)}) copy-start(s32[64,1]{0,1:T(1,128)} %param.15) | copy-start | bytes 772
  13.7 17.1 %copy-start.5 = (s32[12]{0:T(128)S(1)}, s32[12]{0:T(128)}, u32[]{:S(2)}) copy-start(s32[12]{0:T(128)} %param.13) | copy-start | bytes 148
  13.7 660.0 %all-to-all-start = ((f32[16,12,1,128,128]{4,3,1,2,0:T(8,128)}), f32[16,12,1,128,128]{4,3,1,2,0:T(8,128)}, u32[]{:S(2)}, u32[]{:S(2)}) async-start(f32[16,12,1,128,128]{4,3,1,2,0:T(8,128)} %stack.2), calls=%async_computation | async-start | bytes 25165824 | tf_op jit(solution)/shard_map/all_to_all | solution.py:25
  29.3 646.5 %copy-start = (s32[4]{0:T(128)S(1)}, s32[4]{0:T(128)}, u32[]{:S(2)}) copy-start(s32[4]{0:T(128)} %constant.90.clone.1) | copy-start | bytes 52
  29.3 343.7 %all-gather.2.cloned.1.call-start = ((), (), s32[]{:S(2)}) async-start(), calls=%async_computation.1 | async-start | bytes 4325376 | tf_op jit(solution)/shard_map/all_gather | solution.py:13
Sparse Core Ops, SparseCore 0:
  32.2 340.7 all-gather.1
